TPU v7x, 128 devices: a whole 4x4x4 slice. The times are simulated.
128 devices in a mesh: row: 16 (over x, z), col: 8 (over y, core).
Axes of the slice: x: 4, y: 4, z: 4, core: 2. Of those that a mesh axis runs over, the one named last changes fastest.
Arguments:
- tiles: bfloat16 [768, 1024, 1024], P(('row', 'col')), may hold values from -0.1875 to 0.1875
- tile_list: int32 [768, 2], P(('row', 'col')), may hold values from 0 to 63, as said below
- tile_count: int32 [128], P(('row', 'col')), may hold values from 1 to 6, as said below
- scale_index: int32 [768], P(('row', 'col')), may hold values from 0 to 63
- scales: float32 [64], replicated, may hold values from 0.25 to 4
- panel_start: bfloat16 [65536, 128], P(('row', 'col')), may hold values from -6 to 6
- centroids: bfloat16 [4096, 128], replicated, may hold values from -2 to 2
Outputs:
- panel: bfloat16 [65536, 128], P(('row', 'col'))
- centers: float32 [4096, 128], replicated
Inputs may be any that keep to these rules, and one draw needn't show every extreme that they name: `tile_list`: device d holds slots d * 6 to (d + 1) * 6 - 1. With d = i * 8 + j, its tiles lie in row blocks i * 4 to (i + 1) * 4 - 1 and column blocks j * 8 to (j + 1) * 8 - 1, and no two slots of a device name the same block. `tile_count`: live slots of each device; some device fills all its slots.
All inputs are finite; a program needn't handle non-finite values.
Results may differ from a plain program's by a relative error of at most 0.008.
Values may be sent and summed in bfloat16 or wider, within the bound.
No kernel may reach another device: no remote copies, remote signals or barrier semaphores. Data moves between devices by JAX's collectives and lax.ppermute only.
A program may use at most 128 MiB of HBM per device.

v0:
```python
import jax
import jax.numpy as jnp
from jax import lax
from jax.sharding import PartitionSpec as P

ROUNDS = 2
SHARPNESS = 48.0
EPS = 1e-06


def accumulate(
    tiles, source_blocks, target_blocks, weights, live_count, gathered, out_rows, transposed
):
    block_size = tiles.shape[1]

    def add_tile(slot_index, running):
        tile_data = lax.dynamic_index_in_dim(tiles, slot_index, 0, keepdims=False)
        source_rows = lax.dynamic_slice_in_dim(
            gathered, source_blocks[slot_index] * block_size, block_size, 0
        )
        if transposed:
            product_block = lax.dot_general(
                tile_data, source_rows, (((0,), (0,)), ((), ())), preferred_element_type=jnp.float32
            )
        else:
            product_block = jnp.dot(tile_data, source_rows, preferred_element_type=jnp.float32)
        offset = target_blocks[slot_index] * block_size
        current = lax.dynamic_slice_in_dim(running, offset, block_size, 0)
        return lax.dynamic_update_slice_in_dim(
            running, current + weights[slot_index] * product_block, offset, 0
        )

    start_sum = jnp.zeros((out_rows, gathered.shape[1]), jnp.float32)
    return lax.fori_loop(0, live_count, add_tile, start_sum)


def local_gram(product):
    return lax.dot_general(
        product,
        product,
        (((0,), (0,)), ((), ())),
        precision=lax.Precision.HIGHEST,
        preferred_element_type=jnp.float32,
    )


def finish(product, gram_matrix):
    lower_factor = jnp.linalg.cholesky(gram_matrix)
    identity = jnp.eye(product.shape[1], dtype=jnp.float32)
    inverse = lax.linalg.triangular_solve(lower_factor, identity, left_side=True, lower=True)
    return jnp.dot(
        product, inverse.T, precision=lax.Precision.HIGHEST, preferred_element_type=jnp.float32
    ).astype(jnp.bfloat16)


def orthonormal(product, total_rows):
    gram_matrix = lax.psum(local_gram(product), ("row", "col")) / total_rows
    return finish(product, gram_matrix)


def shards(tiles, tile_list, tile_count, scale_index, scales, panel_start, centroids):
    block_size = tiles.shape[1]
    piece_rows = panel_start.shape[0]
    rows_axis = lax.axis_size("row")
    cols_axis = lax.axis_size("col")
    total_rows = piece_rows * rows_axis * cols_axis
    row_at = lax.axis_index("row")
    col_at = lax.axis_index("col")
    range_rows = piece_rows * cols_axis
    range_cols = piece_rows * rows_axis
    local_rows = tile_list[:, 0] - row_at * (range_rows // block_size)
    local_cols = tile_list[:, 1] - col_at * (range_cols // block_size)
    live_count = tile_count[0]
    table_ids = jnp.arange(scales.shape[0], dtype=jnp.int32)
    weights = jnp.sum(
        jnp.where(scale_index[:, None] == table_ids[None, :], scales[None, :], 0.0), axis=1
    )
    panel = panel_start
    for round_index in range(ROUNDS):
        gathered = lax.all_gather(panel, "col", axis=0, tiled=True)
        partial_sum = accumulate(
            tiles, local_rows, local_cols, weights, live_count, gathered, range_cols, True
        )
        product = lax.psum_scatter(partial_sum, "row", scatter_dimension=0, tiled=True)
        factor = orthonormal(product, total_rows)
        gathered = lax.all_gather(factor, "row", axis=0, tiled=True)
        partial_sum = accumulate(
            tiles, local_cols, local_rows, weights, live_count, gathered, range_rows, False
        )
        product = lax.psum_scatter(partial_sum, "col", scatter_dimension=0, tiled=True)
        panel = orthonormal(product, total_rows)
    values = panel.astype(jnp.float32)
    row_norm = jnp.sqrt(jnp.sum(values * values, axis=1, keepdims=True) + EPS)
    points = (values / row_norm).astype(jnp.bfloat16)
    center_values = centroids.astype(jnp.float32)
    center_sq = jnp.sum(center_values * center_values, axis=1)
    affinity = lax.dot_general(
        points, centroids, (((1,), (1,)), ((), ())), preferred_element_type=jnp.float32
    )
    scores = SHARPNESS * (2.0 * affinity - center_sq[None, :])
    shifted = jnp.exp(scores - jnp.max(scores, axis=1, keepdims=True))
    resp = (shifted / jnp.sum(shifted, axis=1, keepdims=True)).astype(jnp.bfloat16)
    sums = lax.dot_general(
        resp, points, (((0,), (0,)), ((), ())), preferred_element_type=jnp.float32
    )
    totals = jnp.sum(resp.astype(jnp.float32), axis=0)
    all_sums, all_totals = lax.psum((sums, totals), ("row", "col"))
    centers = (all_sums + center_values) / (all_totals[:, None] + 1.0)
    return (panel, centers)


def solution(mesh):
    return jax.shard_map(
        shards,
        mesh=mesh,
        in_specs=(
            P(("row", "col"), None, None),
            P(("row", "col"), None),
            P(("row", "col")),
            P(("row", "col")),
            P(),
            P(("row", "col"), None),
            P(),
        ),
        out_specs=(P(("row", "col"), None), P()),
        check_vma=False,
    )
```

profile of v0, /device:TPU:1, one launch (start us, length us, event | category | flops | bytes accessed | tf_op | source)
XLA Modules:
  0.0 1392.8 jit_solution(2792760650536709020)
XLA Ops:
  9.6 27.0 %all-gather.5.cloned.1.call-done = bf16[4096,128]{1,0:T(8,128)(2,1)} async-done(((bf16[512,128]{1,0:T(8,128)(2,1)}), bf16[4096,128]{1,0:T(8,128)(2,1)}) %all-gather.5.cloned.1.call-update) | async-done | bytes 1048592 | tf_op jit(solution)/shard_map/all_gather | solution.py:80
  38.8 8.4 while.40
  47.2 114.8 %reduce-scatter.5.cloned.1.call-done = f32[512,128]{1,0:T(8,128)} async-done(((f32[8192,128]{1,0:T(8,128)}), f32[512,128]{1,0:T(8,128)}) %reduce-scatter.5.cloned.1.call-update) | async-done | bytes 262160 | tf_op jit(solution)/shard_map/reduce_scatter | solution.py:84
  164.3 143.7 %all-reduce.6.cloned.1.call-done = f32[128,128]{0,1:T(8,128)} async-done(((f32[128,128]{0,1:T(8,128)}), f32[128,128]{0,1:T(8,128)}) %all-reduce.6.cloned.1.call-update) | async-done | bytes 65552 | tf_op jit(solution)/shard_map/psum | solution.py:57
  309.8 11.7 cholesky.74
  322.8 9.8 custom-call.8
  335.0 40.4 %all-gather.7.cloned.1.call-done = bf16[8192,128]{1,0:T(8,128)(2,1)} async-done(((bf16[512,128]{1,0:T(8,128)(2,1)}), bf16[8192,128]{1,0:T(8,128)(2,1)}) %all-gather.7.cloned.1.call-update) | async-done | bytes 2097168 | tf_op jit(solution)/shard_map/all_gather | solution.py:86
  384.4 63.8 %reduce-scatter.7.cloned.1.call-done = f32[512,128]{1,0:T(8,128)} async-done(((f32[4096,128]{1,0:T(8,128)}), f32[512,128]{1,0:T(8,128)}) %reduce-scatter.7.cloned.1.call-update) | async-done | bytes 262160 | tf_op jit(solution)/shard_map/reduce_scatter | solution.py:90
  451.0 143.8 %all-reduce.8.cloned.1.call-done = f32[128,128]{0,1:T(8,128)} async-done(((f32[128,128]{0,1:T(8,128)}), f32[128,128]{0,1:T(8,128)}) %all-reduce.8.cloned.1.call-update) | async-done | bytes 65552 | tf_op jit(solution)/shard_map/psum | solution.py:57
  596.6 11.7 cholesky.85
  609.6 9.8 custom-call.9
  621.8 20.6 %all-gather.9.cloned.1.call-done = bf16[4096,128]{1,0:T(8,128)(2,1)} async-done(((bf16[512,128]{1,0:T(8,128)(2,1)}), bf16[4096,128]{1,0:T(8,128)(2,1)}) %all-gather.9.cloned.1.call-update) | async-done | bytes 1048592 | tf_op jit(solution)/shard_map/all_gather | solution.py:80
  644.6 8.3 while.42
  653.0 114.9 %reduce-scatter.9.cloned.1.call-done = f32[512,128]{1,0:T(8,128)} async-done(((f32[8192,128]{1,0:T(8,128)}), f32[512,128]{1,0:T(8,128)}) %reduce-scatter.9.cloned.1.call-update) | async-done | bytes 262160 | tf_op jit(solution)/shard_map/reduce_scatter | solution.py:84
  770.4 143.5 %all-reduce.10.cloned.1.call-done = f32[128,128]{0,1:T(8,128)} async-done(((f32[128,128]{0,1:T(8,128)}), f32[128,128]{0,1:T(8,128)}) %all-reduce.10.cloned.1.call-update) | async-done | bytes 65552 | tf_op jit(solution)/shard_map/psum | solution.py:57
  915.7 11.7 cholesky.96
  928.7 9.8 custom-call.10
  940.9 40.4 %all-gather.11.cloned.1.call-done = bf16[8192,128]{1,0:T(8,128)(2,1)} async-done(((bf16[512,128]{1,0:T(8,128)(2,1)}), bf16[8192,128]{1,0:T(8,128)(2,1)}) %all-gather.11.cloned.1.call-update) | async-done | bytes 2097168 | tf_op jit(solution)/shard_map/all_gather | solution.py:86
  990.4 63.9 %reduce-scatter.11.cloned.1.call-done = f32[512,128]{1,0:T(8,128)} async-done(((f32[4096,128]{1,0:T(8,128)}), f32[512,128]{1,0:T(8,128)}) %reduce-scatter.11.cloned.1.call-update) | async-done | bytes 262160 | tf_op jit(solution)/shard_map/reduce_scatter | solution.py:90
  1057.4 143.4 %all-reduce.12.cloned.1.call-done = f32[128,128]{0,1:T(8,128)} async-done(((f32[128,128]{0,1:T(8,128)}), f32[128,128]{0,1:T(8,128)}) %all-reduce.12.cloned.1.call-update) | async-done | bytes 65552 | tf_op jit(solution)/shard_map/psum | solution.py:57
  1202.6 11.7 cholesky.107
  1215.6 9.8 custom-call.11
  1235.6 64.3 %psum.47 = f32[4096]{0:T(1024)S(1)} all-reduce(f32[4096]{0:T(1024)S(1)} %get-tuple-element.248), channel_id=1, replica_groups=mesh['row'=16,'col'=8] {'row','col'}, use_global_device_ids=true, to_apply=%region_25.28 | all-reduce | flops 4096 | bytes 32768 | tf_op jit(solution)/shard_map/psum | solution.py:107
  1299.9 83.2 %all-reduce.14.cloned.1.call-done = f32[4096,128]{1,0:T(8,128)} async-done(((f32[4096,128]{1,0:T(8,128)}), f32[4096,128]{1,0:T(8,128)}) %all-reduce.14.cloned.1.call-update) | async-done | bytes 2097168 | tf_op jit(solution)/shard_map/psum | solution.py:107
  (101 shorter events, 88.9 us)
Async XLA Ops:
  7.2 29.4 %all-gather.5.cloned.1.call-start = ((), (), s32[]{:S(2)}) async-start(), calls=%async_computation.4 | async-start | bytes 1179648 | tf_op jit(solution)/shard_map/all_gather | solution.py:80
  7.9 154.1 %reduce-scatter.5.cloned.1.call-start = ((), (), s32[]{:S(2)}) async-start(), calls=%async_computation.5 | async-start | bytes 4456448 | tf_op jit(solution)/shard_map/reduce_scatter | solution.py:84
  47.1 260.8 %all-reduce.6.cloned.1.call-start = ((), (), s32[]{:S(2)}) async-start(), calls=%async_computation.6 | async-start | bytes 131072 | tf_op jit(solution)/shard_map/psum | solution.py:57
  164.3 211.2 %all-gather.7.cloned.1.call-start = ((), (), s32[]{:S(2)}) async-start(), calls=%async_computation.7 | async-start | bytes 2228224 | tf_op jit(solution)/shard_map/all_gather | solution.py:86
  335.0 113.2 %reduce-scatter.7.cloned.1.call-start = ((), (), s32[]{:S(2)}) async-start(), calls=%async_computation.8 | async-start | bytes 2359296 | tf_op jit(solution)/shard_map/reduce_scatter | solution.py:90
  383.0 1.3 copy-start.1
  384.3 210.5 %all-reduce.8.cloned.1.call-start = ((), (), s32[]{:S(2)}) async-start(), calls=%async_computation.9 | async-start | bytes 131072 | tf_op jit(solution)/shard_map/psum | solution.py:57
  450.4 192.0 %all-gather.9.cloned.1.call-start = ((), (), s32[]{:S(2)}) async-start(), calls=%async_computation.10 | async-start | bytes 1179648 | tf_op jit(solution)/shard_map/all_gather | solution.py:80
  621.8 146.2 %reduce-scatter.9.cloned.1.call-start = ((), (), s32[]{:S(2)}) async-start(), calls=%async_computation.11 | async-start | bytes 4456448 | tf_op jit(solution)/shard_map/reduce_scatter | solution.py:84
  653.0 260.9 %all-reduce.10.cloned.1.call-start = ((), (), s32[]{:S(2)}) async-start(), calls=%async_computation.12 | async-start | bytes 131072 | tf_op jit(solution)/shard_map/psum | solution.py:57
  770.2 211.2 %all-gather.11.cloned.1.call-start = ((), (), s32[]{:S(2)}) async-start(), calls=%async_computation.13 | async-start | bytes 2228224 | tf_op jit(solution)/shard_map/all_gather | solution.py:86
  940.9 113.4 %reduce-scatter.11.cloned.1.call-start = ((), (), s32[]{:S(2)}) async-start(), calls=%async_computation.14 | async-start | bytes 2359296 | tf_op jit(solution)/shard_map/reduce_scatter | solution.py:90
  981.5 75.3 %copy-start.2 = (bf16[4096,128]{1,0:T(8,128)(2,1)S(1)}, bf16[4096,128]{1,0:T(8,128)(2,1)}, u32[]{:S(2)}) copy-start(bf16[4096,128]{1,0:T(8,128)(2,1)} %param.24) | copy-start | bytes 3145732
  989.0 1.3 copy-start
  990.3 210.5 %all-reduce.12.cloned.1.call-start = ((), (), s32[]{:S(2)}) async-start(), calls=%async_computation.15 | async-start | bytes 131072 | tf_op jit(solution)/shard_map/psum | solution.py:57
  1056.5 326.6 %all-reduce.14.cloned.1.call-start = ((), (), s32[]{:S(2)}) async-start(), calls=%async_computation.16 | async-start | bytes 4194304 | tf_op jit(solution)/shard_map/psum | solution.py:107
Sparse Core Ops, SparseCore 0:
  9.7 26.8 all-gather.4
  47.3 114.6 reduce-scatter.4
  167.3 140.6 all-reduce.5
  335.1 40.3 all-gather.6
  384.4 63.6 reduce-scatter.6
  453.3 141.4 all-reduce.7
  621.9 20.4 all-gather.8
  653.1 114.7 reduce-scatter.8
  773.2 140.6 all-reduce.9
  941.0 40.3 all-gather.10
  990.4 63.7 reduce-scatter.10
  1059.4 141.3 all-reduce.11
  1234.9 148.1 all-reduce.13
where the time goes:
time: 1400 us; the launch traced here: 1390 us
  waiting for transfers between devices  1140 us (81%)
  other arithmetic  107 us (8%)
  blocking collectives  64.3 us (5%)
  matrix products  35.3 us (3%)
  local copies, waits for them, and re-layouts  15.5 us (1%)
  between operations  14.4 us (1%)
    psum x4, waiting for transfers between devices, orthonormal(): gram_matrix = lax.psum(local_gram(product), ('row', 'col')) / total_rows  574 us
    reduce_scatter x2, waiting for transfers between devices, shards(): lax.psum_scatter(partial_sum, 'row', scatter_dimension=0, tiled=True)  230 us
    reduce_scatter x2, waiting for transfers between devices, shards(): lax.psum_scatter(partial_sum, 'col', scatter_dimension=0, tiled=True)  128 us
    psum x1, waiting for transfers between devices, shards(): all_sums, all_totals = lax.psum((sums, totals), ('row', 'col'))  83.2 us
    all_gather x2, waiting for transfers between devices, shards(): gathered = lax.all_gather(factor, 'row', axis=0, tiled=True)  80.9 us
    psum x1, blocking collectives, shards(): all_sums, all_totals = lax.psum((sums, totals), ('row', 'col'))  64.3 us
    another operation x12, other arithmetic, finish(): lower_factor = jnp.linalg.cholesky(gram_matrix)  49.6 us
    all_gather x2, waiting for transfers between devices, shards(): gathered = lax.all_gather(panel, 'col', axis=0, tiled=True)  47.6 us
  transfers between devices with their start and end apart: 13, of which 13 were waited for; matrix products, arithmetic and copies ran while one was open for 0% of the time, Pallas kernels for 0%

commit v1 on v0

--- a/solution.py
+++ b/solution.py
@@ -54,7 +54,7 @@
 
 
 def orthonormal(product, total_rows):
-    gram_matrix = lax.psum(local_gram(product), ("row", "col")) / total_rows
+    gram_matrix = jnp.sum(lax.all_gather(local_gram(product), ("row", "col")), axis=0) / total_rows
     return finish(product, gram_matrix)
 
 

time: 1400 us -> 1120 us (0.80)
  waiting for transfers between devices: 1140 us -> 860 us
    psum x4 -> x0, waiting for transfers between devices: 574 us -> none  [orthonormal(): gram_matrix = lax.psum(local_gram(product), ('row', 'col')) / total_rows]
    all_gather x0 -> x4, waiting for transfers between devices: none -> 288 us  [orthonormal(): lax.all_gather(local_gram(product), ('row', 'col'))]
    reduce_sum x0 -> x4, other arithmetic: none -> 15.4 us  [orthonormal(): jnp.sum(lax.all_gather(local_gram(product), ('row', 'col')), axis=0)]
where the time goes in v1:
time: 1120 us; the launch traced here: 1110 us
  waiting for transfers between devices  860 us (77%)
  other arithmetic  116 us (10%)
  blocking collectives  63.2 us (6%)
  matrix products  31.6 us (3%)
  local copies, waits for them, and re-layouts  15.8 us (1%)
  between operations  14.5 us (1%)
    all_gather x4, waiting for transfers between devices, orthonormal(): lax.all_gather(local_gram(product), ('row', 'col'))  288 us
    reduce_scatter x2, waiting for transfers between devices, shards(): lax.psum_scatter(partial_sum, 'row', scatter_dimension=0, tiled=True)  230 us
    reduce_scatter x2, waiting for transfers between devices, shards(): lax.psum_scatter(partial_sum, 'col', scatter_dimension=0, tiled=True)  128 us
    psum x1, waiting for transfers between devices, shards(): all_sums, all_totals = lax.psum((sums, totals), ('row', 'col'))  84.5 us
    all_gather x2, waiting for transfers between devices, shards(): gathered = lax.all_gather(factor, 'row', axis=0, tiled=True)  81.3 us
    psum x1, blocking collectives, shards(): all_sums, all_totals = lax.psum((sums, totals), ('row', 'col'))  63.2 us
    another operation x12, other arithmetic, finish(): lower_factor = jnp.linalg.cholesky(gram_matrix)  49.6 us
    all_gather x2, waiting for transfers between devices, shards(): gathered = lax.all_gather(panel, 'col', axis=0, tiled=True)  47.8 us
  transfers between devices with their start and end apart: 13, of which 13 were waited for; matrix products, arithmetic and copies ran while one was open for 0% of the time, Pallas kernels for 0%

profile of v1, /device:TPU:1, one launch (start us, length us, event | category | flops | bytes accessed | tf_op | source)
XLA Modules:
  0.0 1113.0 jit_solution(1976051583285114797)
XLA Ops:
  9.6 27.0 %all-gather.13.cloned.1.call-done = bf16[4096,128]{1,0:T(8,128)(2,1)} async-done(((bf16[512,128]{1,0:T(8,128)(2,1)}), bf16[4096,128]{1,0:T(8,128)(2,1)}) %all-gather.13.cloned.1.call-update) | async-done | bytes 1048592 | tf_op jit(solution)/shard_map/all_gather | solution.py:80
  38.8 8.4 while.40
  47.2 114.8 %reduce-scatter.5.cloned.1.call-done = f32[512,128]{1,0:T(8,128)} async-done(((f32[8192,128]{1,0:T(8,128)}), f32[512,128]{1,0:T(8,128)}) %reduce-scatter.5.cloned.1.call-update) | async-done | bytes 262160 | tf_op jit(solution)/shard_map/reduce_scatter | solution.py:84
  164.3 72.2 %all-gather.21.cloned.1.call-done = f32[16384,128]{1,0:T(8,128)} async-done(((f32[128,128]{1,0:T(8,128)}), f32[16384,128]{1,0:T(8,128)}) %all-gather.21.cloned.1.call-update) | async-done | bytes 8388624 | tf_op jit(solution)/shard_map/all_gather | solution.py:57
  240.6 11.7 %cholesky.74 = f32[128,128]{1,0:T(8,128)S(1)} custom-call(f32[128,128]{1,0:T(8,128)S(1)} %fusion.80), custom_call_target="Cholesky" | custom-call | tf_op jit(solution)/shard_map/jit(cholesky)/cholesky | solution.py:48
  253.6 9.8 custom-call.8
  264.9 40.6 %all-gather.15.cloned.1.call-done = bf16[8192,128]{1,0:T(8,128)(2,1)} async-done(((bf16[512,128]{1,0:T(8,128)(2,1)}), bf16[8192,128]{1,0:T(8,128)(2,1)}) %all-gather.15.cloned.1.call-update) | async-done | bytes 2097168 | tf_op jit(solution)/shard_map/all_gather | solution.py:86
  314.4 63.8 %reduce-scatter.7.cloned.1.call-done = f32[512,128]{1,0:T(8,128)} async-done(((f32[4096,128]{1,0:T(8,128)}), f32[512,128]{1,0:T(8,128)}) %reduce-scatter.7.cloned.1.call-update) | async-done | bytes 262160 | tf_op jit(solution)/shard_map/reduce_scatter | solution.py:90
  381.0 72.3 %all-gather.23.cloned.1.call-done = f32[16384,128]{1,0:T(8,128)} async-done(((f32[128,128]{1,0:T(8,128)}), f32[16384,128]{1,0:T(8,128)}) %all-gather.23.cloned.1.call-update) | async-done | bytes 8388624 | tf_op jit(solution)/shard_map/all_gather | solution.py:57
  457.4 11.7 %cholesky.85 = f32[128,128]{1,0:T(8,128)S(1)} custom-call(f32[128,128]{1,0:T(8,128)S(1)} %fusion.78), custom_call_target="Cholesky" | custom-call | tf_op jit(solution)/shard_map/jit(cholesky)/cholesky | solution.py:48
  470.5 9.8 custom-call.9
  481.7 20.8 %all-gather.17.cloned.1.call-done = bf16[4096,128]{1,0:T(8,128)(2,1)} async-done(((bf16[512,128]{1,0:T(8,128)(2,1)}), bf16[4096,128]{1,0:T(8,128)(2,1)}) %all-gather.17.cloned.1.call-update) | async-done | bytes 1048592 | tf_op jit(solution)/shard_map/all_gather | solution.py:80
  504.7 8.3 while.42
  513.1 114.8 %reduce-scatter.9.cloned.1.call-done = f32[512,128]{1,0:T(8,128)} async-done(((f32[8192,128]{1,0:T(8,128)}), f32[512,128]{1,0:T(8,128)}) %reduce-scatter.9.cloned.1.call-update) | async-done | bytes 262160 | tf_op jit(solution)/shard_map/reduce_scatter | solution.py:84
  630.5 72.0 %all-gather.25.cloned.1.call-done = f32[16384,128]{1,0:T(8,128)} async-done(((f32[128,128]{1,0:T(8,128)}), f32[16384,128]{1,0:T(8,128)}) %all-gather.25.cloned.1.call-update) | async-done | bytes 8388624 | tf_op jit(solution)/shard_map/all_gather | solution.py:57
  706.6 11.7 %cholesky.96 = f32[128,128]{1,0:T(8,128)S(1)} custom-call(f32[128,128]{1,0:T(8,128)S(1)} %fusion.76), custom_call_target="Cholesky" | custom-call | tf_op jit(solution)/shard_map/jit(cholesky)/cholesky | solution.py:48
  719.6 9.8 custom-call.10
  730.9 40.6 %all-gather.19.cloned.1.call-done = bf16[8192,128]{1,0:T(8,128)(2,1)} async-done(((bf16[512,128]{1,0:T(8,128)(2,1)}), bf16[8192,128]{1,0:T(8,128)(2,1)}) %all-gather.19.cloned.1.call-update) | async-done | bytes 2097168 | tf_op jit(solution)/shard_map/all_gather | solution.py:86
  780.5 63.8 %reduce-scatter.11.cloned.1.call-done = f32[512,128]{1,0:T(8,128)} async-done(((f32[4096,128]{1,0:T(8,128)}), f32[512,128]{1,0:T(8,128)}) %reduce-scatter.11.cloned.1.call-update) | async-done | bytes 262160 | tf_op jit(solution)/shard_map/reduce_scatter | solution.py:90
  847.5 72.0 %all-gather.27.cloned.1.call-done = f32[16384,128]{1,0:T(8,128)} async-done(((f32[128,128]{1,0:T(8,128)}), f32[16384,128]{1,0:T(8,128)}) %all-gather.27.cloned.1.call-update) | async-done | bytes 8388624 | tf_op jit(solution)/shard_map/all_gather | solution.py:57
  923.6 11.7 %cholesky.107 = f32[128,128]{1,0:T(8,128)S(1)} custom-call(f32[128,128]{1,0:T(8,128)S(1)} %fusion.74), custom_call_target="Cholesky" | custom-call | tf_op jit(solution)/shard_map/jit(cholesky)/cholesky | solution.py:48
  936.6 9.8 custom-call.11
  955.6 63.2 %psum.15 = f32[4096]{0:T(1024)S(1)} all-reduce(f32[4096]{0:T(1024)S(1)} %get-tuple-element.250), channel_id=1, replica_groups=mesh['row'=16,'col'=8] {'row','col'}, use_global_device_ids=true, to_apply=%region_25.28 | all-reduce | flops 4096 | bytes 32768 | tf_op jit(solution)/shard_map/psum | solution.py:107
  1018.8 84.5 %all-reduce.2.cloned.1.call-done = f32[4096,128]{1,0:T(8,128)} async-done(((f32[4096,128]{1,0:T(8,128)}), f32[4096,128]{1,0:T(8,128)}) %all-reduce.2.cloned.1.call-update) | async-done | bytes 2097168 | tf_op jit(solution)/shard_map/psum | solution.py:107
  (117 shorter events, 94.2 us)
Async XLA Ops:
  7.2 29.4 %all-gather.13.cloned.1.call-start = ((), (), s32[]{:S(2)}) async-start(), calls=%async_computation.4 | async-start | bytes 1179648 | tf_op jit(solution)/shard_map/all_gather | solution.py:80
  7.9 154.1 %reduce-scatter.5.cloned.1.call-start = ((), (), s32[]{:S(2)}) async-start(), calls=%async_computation.5 | async-start | bytes 4456448 | tf_op jit(solution)/shard_map/reduce_scatter | solution.py:84
  47.1 189.3 %all-gather.21.cloned.1.call-start = ((), (), s32[]{:S(2)}) async-start(), calls=%async_computation.13 | async-start | bytes 8454144 | tf_op jit(solution)/shard_map/all_gather | solution.py:57
  164.3 141.2 %all-gather.15.cloned.1.call-start = ((), (), s32[]{:S(2)}) async-start(), calls=%async_computation.6 | async-start | bytes 2228224 | tf_op jit(solution)/shard_map/all_gather | solution.py:86
  236.5 27.2 %copy-start.4 = (f32[512,128]{1,0:T(8,128)S(1)}, f32[512,128]{1,0:T(8,128)}, u32[]{:S(2)}) copy-start(f32[512,128]{1,0:T(8,128)} %reduce-scatter.5.cloned.1.call-done) | copy-start | bytes 786436
  264.8 113.4 %reduce-scatter.7.cloned.1.call-start = ((), (), s32[]{:S(2)}) async-start(), calls=%async_computation.7 | async-start | bytes 2359296 | tf_op jit(solution)/shard_map/reduce_scatter | solution.py:90
  313.0 1.3 copy-start
  314.4 139.0 %all-gather.23.cloned.1.call-start = ((), (), s32[]{:S(2)}) async-start(), calls=%async_computation.14 | async-start | bytes 8454144 | tf_op jit(solution)/shard_map/all_gather | solution.py:57
  380.5 122.0 %all-gather.17.cloned.1.call-start = ((), (), s32[]{:S(2)}) async-start(), calls=%async_computation.8 | async-start | bytes 1179648 | tf_op jit(solution)/shard_map/all_gather | solution.py:80
  453.3 27.2 %copy-start.5 = (f32[512,128]{1,0:T(8,128)S(1)}, f32[512,128]{1,0:T(8,128)}, u32[]{:S(2)}) copy-start(f32[512,128]{1,0:T(8,128)} %reduce-scatter.7.cloned.1.call-done) | copy-start | bytes 786436
  481.7 146.3 %reduce-scatter.9.cloned.1.call-start = ((), (), s32[]{:S(2)}) async-start(), calls=%async_computation.9 | async-start | bytes 4456448 | tf_op jit(solution)/shard_map/reduce_scatter | solution.py:84
  513.1 189.4 %all-gather.25.cloned.1.call-start = ((), (), s32[]{:S(2)}) async-start(), calls=%async_computation.15 | async-start | bytes 8454144 | tf_op jit(solution)/shard_map/all_gather | solution.py:57
  630.3 141.2 %all-gather.19.cloned.1.call-start = ((), (), s32[]{:S(2)}) async-start(), calls=%async_computation.10 | async-start | bytes 2228224 | tf_op jit(solution)/shard_map/all_gather | solution.py:86
  702.5 27.2 %copy-start.6 = (f32[512,128]{1,0:T(8,128)S(1)}, f32[512,128]{1,0:T(8,128)}, u32[]{:S(2)}) copy-start(f32[512,128]{1,0:T(8,128)} %reduce-scatter.9.cloned.1.call-done) | copy-start | bytes 786436
  730.8 113.5 %reduce-scatter.11.cloned.1.call-start = ((), (), s32[]{:S(2)}) async-start(), calls=%async_computation.11 | async-start | bytes 2359296 | tf_op jit(solution)/shard_map/reduce_scatter | solution.py:90
  771.6 75.2 %copy-start.2 = (bf16[4096,128]{1,0:T(8,128)(2,1)S(1)}, bf16[4096,128]{1,0:T(8,128)(2,1)}, u32[]{:S(2)}) copy-start(bf16[4096,128]{1,0:T(8,128)(2,1)} %param.24) | copy-start | bytes 3145732
  779.1 1.3 copy-start.1
  780.5 139.0 %all-gather.27.cloned.1.call-start = ((), (), s32[]{:S(2)}) async-start(), calls=%async_computation.16 | async-start | bytes 8454144 | tf_op jit(solution)/shard_map/all_gather | solution.py:57
  846.6 256.7 %all-reduce.2.cloned.1.call-start = ((), (), s32[]{:S(2)}) async-start(), calls=%async_computation.12 | async-start | bytes 4194304 | tf_op jit(solution)/shard_map/psum | solution.py:107
  919.5 27.2 %copy-start.3 = (f32[512,128]{1,0:T(8,128)S(1)}, f32[512,128]{1,0:T(8,128)}, u32[]{:S(2)}) copy-start(f32[512,128]{1,0:T(8,128)} %reduce-scatter.11.cloned.1.call-done) | copy-start | bytes 786436
Sparse Core Ops, SparseCore 0:
  9.7 26.8 all-gather.12
  47.3 114.6 reduce-scatter.4
  165.5 70.9 all-gather.20
  264.9 40.5 all-gather.14
  314.5 63.6 reduce-scatter.6
  381.6 71.6 all-gather.22
  481.8 20.6 all-gather.16
  513.2 114.7 reduce-scatter.8
  631.5 70.9 all-gather.24
  730.9 40.5 all-gather.18
  780.6 63.6 reduce-scatter.10
  847.7 71.6 all-gather.26
  955.0 148.2 all-reduce.1
